TPU v7x, 32 devices: a whole 2x2x4 slice. The times are simulated.
32 devices in a mesh: pb: 8 (over z, y), ka: 4 (over x, core).
Axes of the slice: x: 2, y: 2, z: 4, core: 2. Of those that a mesh axis runs over, the one named last changes fastest.
Arguments:
- query_rows: bfloat16 [4096, 512], P(('pb', 'ka')), may hold values from -8 to 8
- key_rows: bfloat16 [4096, 128], P(('pb', 'ka')), may hold values from -3 to 3
- value_rows: bfloat16 [4096, 128], P(('pb', 'ka')), may hold values from -6 to 6
- outputs: bfloat16 [4096, 512], P(('pb', 'ka')), may hold values from -3 to 3
- out_grads: bfloat16 [4096, 512], P(('pb', 'ka')), may hold values from -6 to 6
- log_totals: float32 [4, 4096], P(None, ('pb', 'ka'))
- selected: int32 [32, 2], P(('pb', 'ka')), may hold values from 0 to 31, as said below
- counts: int32 [32], P(('pb', 'ka')), may hold values from 1 to 2, as said below
Outputs:
- query_grad: float32 [4096, 512], P(('pb', 'ka'))
- key_grad: float32 [4096, 128], P(('pb', 'ka'))
- value_grad: float32 [4096, 128], P(('pb', 'ka'))
Inputs may be any that keep to these rules, and one draw needn't show every extreme that they name: `selected`: slot 0 of row q is q itself; the first counts[q] entries of row q are distinct blocks no later than q; entries from slot counts[q] on are padding and are ignored. counts[q] is at most q + 1; the last query block's count is 2.
All inputs are finite; a program needn't handle non-finite values.
Results may differ from a plain program's by a relative error of at most 0.0029.
Values may be sent and summed in bfloat16 or wider, within the bound.
A program may use at most 64 MiB of HBM per device.

v0:
```python
import jax
import jax.numpy as jnp
from jax import lax
from jax.sharding import PartitionSpec as P

VERY_LOW = -1e30


def passed_along(value, axis, steps):
    count = lax.axis_size(axis)
    pairs = [(source, (source + steps) % count) for source in range(count)]
    return lax.ppermute(value, axis, pairs)


def head_sums(grad_rows, out_rows, head_width):
    row_total = grad_rows.shape[0]
    part_heads = grad_rows.shape[1] // head_width
    product = grad_rows.astype(jnp.float32) * out_rows.astype(jnp.float32)
    return jnp.sum(product.reshape(row_total, part_heads, head_width), axis=2).T


def shards(query_rows, key_rows, value_rows, outputs, out_grads, log_totals, selected, counts):
    ka_count = lax.axis_size("ka")
    ka_index = lax.axis_index("ka")
    pb_index = lax.axis_index("pb")
    block_count = selected.shape[0]
    slot_count = selected.shape[1]
    head_width = key_rows.shape[1]
    block_rows = query_rows.shape[0] // block_count
    score_scale = head_width ** (-0.5)
    key_pairs = jnp.concatenate([key_rows, value_rows], 1)
    column_keys = lax.all_gather(key_pairs, "pb", axis=0, tiled=True)
    peer_slots, peer_counts = (
        lax.all_gather(selected, "ka", axis=0, tiled=True),
        lax.all_gather(counts, "ka", axis=0, tiled=True),
    )
    key_grads = jnp.zeros((column_keys.shape[0], 2 * head_width), jnp.float32)
    row_offsets = jnp.arange(block_rows, dtype=jnp.int32)
    flat_owner = jnp.repeat(jnp.arange(block_count, dtype=jnp.int32), slot_count)
    flat_slot = jnp.tile(jnp.arange(slot_count, dtype=jnp.int32), block_count)
    flat_places = jnp.arange(block_count * slot_count, dtype=jnp.int32)

    def visit_block(row_stack, query_grad, stat_stack, anchor, key_grads):
        held_query = row_stack[0]
        held_grad = row_stack[1]
        total_rows = stat_stack[0]
        delta_rows = head_sums(row_stack[1], row_stack[2], head_width)
        part_heads = total_rows.shape[0]
        held_slots = lax.dynamic_slice_in_dim(
            peer_slots, anchor * block_count, block_count, 0
        ).reshape(-1)
        held_counts = jnp.repeat(
            lax.dynamic_slice_in_dim(peer_counts, anchor * block_count, block_count, 0), slot_count
        )
        first_block = (pb_index * ka_count + anchor) * block_count
        wanted = (flat_slot < held_counts) & (held_slots // block_count % ka_count == ka_index)
        position = jnp.cumsum(wanted.astype(jnp.int32)) - 1
        placed = wanted[:, None] & (position[:, None] == flat_places[None, :])
        packed_ids = jnp.sum(jnp.where(placed, held_slots[:, None], 0), axis=0)
        packed_owner = jnp.sum(jnp.where(placed, flat_owner[:, None], 0), axis=0)
        live_tiles = jnp.sum(wanted.astype(jnp.int32))

        def one_tile(tile_index, loop_state):
            query_grad, key_grads = loop_state
            key_block = packed_ids[tile_index]
            owner_block = packed_owner[tile_index]
            key_start = (
                key_block // (block_count * ka_count) * block_count + key_block % block_count
            ) * block_rows
            pair_tile = lax.dynamic_slice_in_dim(column_keys, key_start, block_rows, 0)
            key_tile = pair_tile[:, :head_width]
            value_tile = pair_tile[:, head_width:]
            query_tile = held_query.reshape(block_rows, part_heads, head_width)
            grad_tile = held_grad.reshape(block_rows, part_heads, head_width)
            scores = (
                jnp.einsum("rhd,cd->hrc", query_tile, key_tile, preferred_element_type=jnp.float32)
                * score_scale
            )
            query_pos = (first_block + owner_block) * block_rows + row_offsets
            key_pos = key_block * block_rows + row_offsets
            allowed = key_pos[None, :] <= query_pos[:, None]
            probs_full = jnp.exp(
                jnp.where(allowed[None], scores - total_rows[:, :, None], VERY_LOW)
            )
            prob_grads = jnp.einsum(
                "rhd,cd->hrc", grad_tile, value_tile, preferred_element_type=jnp.float32
            )
            score_grads = probs_full * (prob_grads - delta_rows[:, :, None])
            rounded_probs = probs_full.astype(jnp.bfloat16)
            rounded_grads = score_grads.astype(jnp.bfloat16)
            value_part = jnp.einsum(
                "hrc,rhd->cd", rounded_probs, grad_tile, preferred_element_type=jnp.float32
            )
            key_part = (
                jnp.einsum(
                    "hrc,rhd->cd", rounded_grads, query_tile, preferred_element_type=jnp.float32
                )
                * score_scale
            )
            query_part = (
                jnp.einsum(
                    "hrc,cd->rhd", rounded_grads, key_tile, preferred_element_type=jnp.float32
                )
                * score_scale
            )
            old_query = query_grad
            query_grad = old_query + query_part.reshape(block_rows, -1)
            old_keys = lax.dynamic_slice_in_dim(key_grads, key_start, block_rows, 0)
            key_grads = lax.dynamic_update_slice_in_dim(
                key_grads, old_keys + jnp.concatenate([key_part, value_part], 1), key_start, 0
            )
            return (query_grad, key_grads)

        return lax.fori_loop(0, live_tiles, one_tile, (query_grad, key_grads))

    query_part = query_rows
    grad_zero = jnp.zeros(query_part.shape, jnp.float32)
    row_stack = jnp.stack([query_part, out_grads, outputs])
    query_grad = grad_zero
    stat_stack = log_totals[None]

    def forward_hop(hop_index, loop_state):
        row_stack, query_grad, stat_stack, key_grads = loop_state
        anchor = (ka_index - hop_index) % ka_count
        query_grad, key_grads = visit_block(row_stack, query_grad, stat_stack, anchor, key_grads)
        row_stack = passed_along(row_stack, "ka", 1)
        query_grad, stat_stack = passed_along((query_grad, stat_stack), "ka", 1)
        return (row_stack, query_grad, stat_stack, key_grads)

    row_stack, query_grad, stat_stack, key_grads = lax.fori_loop(
        0, ka_count - 1, forward_hop, (row_stack, query_grad, stat_stack, key_grads)
    )
    query_grad, key_grads = visit_block(
        row_stack, query_grad, stat_stack, (ka_index + 1) % ka_count, key_grads
    )
    query_grad = passed_along(query_grad, "ka", 1)
    owned_grads = lax.psum_scatter(key_grads, "pb", scatter_dimension=0, tiled=True)
    return (query_grad, owned_grads[:, :head_width], owned_grads[:, head_width:])


def solution(mesh):
    return jax.shard_map(
        shards,
        mesh=mesh,
        in_specs=(
            P(("pb", "ka"), None),
            P(("pb", "ka"), None),
            P(("pb", "ka"), None),
            P(("pb", "ka"), None),
            P(("pb", "ka"), None),
            P(None, ("pb", "ka")),
            P(("pb", "ka"), None),
            P(("pb", "ka")),
        ),
        out_specs=(P(("pb", "ka"), None), P(("pb", "ka"), None), P(("pb", "ka"), None)),
        check_vma=False,
    )
```

profile of v0, /device:TPU:0, one launch (start us, length us, event | category | flops | bytes accessed | tf_op | source)
XLA Modules:
  0.0 183.4 jit_solution(7212830723820672716)
XLA Ops:
  8.5 0.7 dynamic-slice
  9.2 0.8 dynamic-update-slice
  10.0 6.4 %all-reduce = s32[4]{0:T(128)S(1)} all-reduce(s32[4]{0:T(128)S(1)} %dynamic-update-slice), channel_id=1, replica_groups=mesh['pb'=8,'ka'=4] {'ka'}, use_global_device_ids=true, to_apply=%add | all-reduce | flops 4 | bytes 32
  16.4 0.7 copy-done.5
  17.0 5.0 %all-gather = s32[4,1,2]{2,1,0:T(1,128)S(1)} all-gather(s32[1,1,2]{2,1,0:T(1,128)S(1)} %bitcast.222), channel_id=1, replica_groups=mesh['pb'=8,'ka'=4] {'ka'}, dimensions={0}, use_global_device_ids=true | all-gather | bytes 40 | tf_op jit(solution)/shard_map/all_gather | solution.py:34
  22.7 1.3 convert_reduce_fusion.1
  24.5 1.1 copy.63
  25.7 0.8 copy-done.2
  27.3 31.9 %all_gather.11 = bf16[1024,256]{1,0:T(8,128)(2,1)S(1)} all-gather(bf16[128,256]{1,0:T(8,128)(2,1)S(1)} %pad_maximum_fusion.1), channel_id=1, replica_groups=mesh['pb'=8,'ka'=4] {'pb'}, dimensions={0}, use_global_device_ids=true | all-gather | bytes 589824 | tf_op jit(solution)/shard_map/all_gather | solution.py:32
  60.0 40.6 %while.86 = (s32[]{:T(128)}, bf16[3,128,512]{1,2,0:T(8,128)(2,1)S(1)}, f32[128,512]{0,1:T(8,128)S(1)}, f32[1,4,128]{2,1,0:T(4,128)S(1)}, f32[1024,256]{0,1:T(8,1...) while((s32[]{:T(128)}, ...), condition=%wide.region_7.8_spmd.clone.clone, body=%wide.region_0.7_spmd.clone.clone.sunk | while | flops 84836216 | bytes 8673559 | solution.py:130
  60.1 0.7 dynamic_slice.117
  60.7 1.3 convert_reduce_fusion.3
  62.0 0.6 fusion.81
  63.1 6.2 %while.88 = (s32[]{:T(128)}, f32[128,512]{0,1:T(8,128)S(1)}, f32[1024,256]{0,1:T(8,128)S(1)}, s32[]{:T(128)}, s32[2]{0:T(128)S(1)}, /*index=5*/bf16[1024,256]{1,...) while((s32[]{:T(128)}, f32[128,512]{0,1:T(8,128)S(1)}, ...), condition=%wide.region_6.6_spmd.clone, body=%wide.region_5.5_spmd.clone.sunk | while | flops 84574488 | bytes 3415011 | solution.py:114
  69.3 1.0 collective-permute-start.1
  70.3 4.8 %collective-permute-done.1 = f32[128,512]{0,1:T(8,128)S(1)} collective-permute-done((f32[128,512]{0,1:T(8,128)S(1)}, f32[128,512]{0,1:T(8,128)S(1)}, u32[]{:S(2)}, u32[]{:S(2)}) %collective-permute-start.1) | collective-permute-done | bytes 262176 | tf_op jit(solution)/shard_map/while/body/eval_jaxpr/ppermute | solution.py:12
  75.3 0.7 dynamic_slice.117
  76.0 1.3 convert_reduce_fusion.3
  78.9 1.0 collective-permute-start.1
  80.0 5.3 %collective-permute-done.1 = f32[128,512]{0,1:T(8,128)S(1)} collective-permute-done((f32[128,512]{0,1:T(8,128)S(1)}, f32[128,512]{0,1:T(8,128)S(1)}, u32[]{:S(2)}, u32[]{:S(2)}) %collective-permute-start.1) | collective-permute-done | bytes 262176 | tf_op jit(solution)/shard_map/while/body/eval_jaxpr/ppermute | solution.py:12
  85.5 0.7 dynamic_slice.117
  86.1 1.3 convert_reduce_fusion.3
  87.4 0.6 fusion.81
  88.4 6.2 %while.88 = (s32[]{:T(128)}, f32[128,512]{0,1:T(8,128)S(1)}, f32[1024,256]{0,1:T(8,128)S(1)}, s32[]{:T(128)}, s32[2]{0:T(128)S(1)}, /*index=5*/bf16[1024,256]{1,...) while((s32[]{:T(128)}, f32[128,512]{0,1:T(8,128)S(1)}, ...), condition=%wide.region_6.6_spmd.clone, body=%wide.region_5.5_spmd.clone.sunk | while | flops 84574488 | bytes 3415011 | solution.py:114
  94.7 1.0 collective-permute-start.1
  95.7 4.8 %collective-permute-done.1 = f32[128,512]{0,1:T(8,128)S(1)} collective-permute-done((f32[128,512]{0,1:T(8,128)S(1)}, f32[128,512]{0,1:T(8,128)S(1)}, u32[]{:S(2)}, u32[]{:S(2)}) %collective-permute-start.1) | collective-permute-done | bytes 262176 | tf_op jit(solution)/shard_map/while/body/eval_jaxpr/ppermute | solution.py:12
  100.9 6.4 %while.87 = (s32[]{:T(128)}, f32[128,512]{0,1:T(8,128)S(1)}, f32[1024,256]{0,1:T(8,128)S(1)}, s32[]{:T(128)}, s32[2]{0:T(128)S(1)}, /*index=5*/bf16[1024,256]{1,...) while((s32[]{:T(128)}, f32[128,512]{0,1:T(8,128)S(1)}, ...), condition=%wide.region_13.14_spmd.clone.clone, body=%wide.region_12.13_spmd.clone.clone.sunk | while | flops 84574488 | bytes 3414491 | solution.py:114
  107.4 1.3 copy.67
  108.9 5.8 %collective-permute-done.3 = f32[128,512]{1,0:T(8,128)S(1)} collective-permute-done((f32[128,512]{1,0:T(8,128)S(1)}, f32[128,512]{1,0:T(8,128)S(1)}, u32[]{:S(2)}, u32[]{:S(2)}) %collective-permute-start.3) | collective-permute-done | bytes 262176 | tf_op jit(solution)/shard_map/ppermute | solution.py:12
  114.7 59.6 %reduce-scatter.2.cloned.1.call-done = f32[128,256]{1,0:T(8,128)} async-done(((f32[1024,256]{1,0:T(8,128)}), f32[128,256]{1,0:T(8,128)}) %reduce-scatter.2.cloned.1.call-update) | async-done | bytes 131088 | tf_op jit(solution)/shard_map/reduce_scatter | solution.py:137
  174.3 1.5 fusion.43
  175.8 0.7 copy.125
  (105 shorter events, 12.1 us)
Async XLA Ops:
  7.2 167.1 %reduce-scatter.2.cloned.1.call-start = ((), (), s32[]{:S(2)}) async-start(), calls=%async_computation.1 | async-start | bytes 1179648 | tf_op jit(solution)/shard_map/reduce_scatter | solution.py:137
  7.9 0.7 copy-start.6
  16.4 0.7 copy-start.5
  24.5 1.1 copy-start.1
  25.6 0.9 copy-start.2
  26.5 0.8 copy-start.3
  26.5 0.8 copy-start.4
  59.3 0.7 copy-start
  60.0 15.2 %collective-permute-start = (bf16[3,128,512]{1,2,0:T(8,128)(2,1)S(1)}, bf16[3,128,512]{1,2,0:T(8,128)(2,1)S(1)}, u32[]{:S(2)}, u32[]{:S(2)}) collective-permute-start(bf16[3,128,512]{1,2,0:T(8,128)(2,1)S(1)} %copy.101), channel_id=1, source_target_pairs={{0,1},{1,2},{2,3},{3,0},{4,5},{5,6},{6,7},{7,4},{8,9},{9,10},{10,1... | collective-permute-start | bytes 1179656 | tf_op jit(solution)/shard_map/while/body/eval_jaxpr/ppermute | solution.py:12
  69.3 5.8 %collective-permute-start.1 = (f32[128,512]{0,1:T(8,128)S(1)}, f32[128,512]{0,1:T(8,128)S(1)}, u32[]{:S(2)}, u32[]{:S(2)}) collective-permute-start(f32[128,512]{0,1:T(8,128)S(1)} %get-tuple-element.1444), channel_id=1, source_target_pairs={{0,1},{1,2},{2,3},{3,0},{4,5},{5,6},{6,7},{7,4},{8,9},{9,10},{10,1... | collective-permute-start | bytes 786440 | tf_op jit(solution)/shard_map/while/body/eval_jaxpr/ppermute | solution.py:12
  70.3 4.9 %collective-permute-start.2 = (f32[1,4,128]{2,1,0:T(4,128)S(1)}, f32[1,4,128]{2,1,0:T(4,128)S(1)}, u32[]{:S(2)}, u32[]{:S(2)}) collective-permute-start(f32[1,4,128]{2,1,0:T(4,128)S(1)} %get-tuple-element.1678), channel_id=1, source_target_pairs={{0,1},{1,2},{2,3},{3,0},{4,5},{5,6},{6,7},{7,4},{8,9},{9,10},{10,1... | collective-permute-start | bytes 6152 | tf_op jit(solution)/shard_map/while/body/eval_jaxpr/ppermute | solution.py:12
  75.2 10.1 %collective-permute-start = (bf16[3,128,512]{1,2,0:T(8,128)(2,1)S(1)}, bf16[3,128,512]{1,2,0:T(8,128)(2,1)S(1)}, u32[]{:S(2)}, u32[]{:S(2)}) collective-permute-start(bf16[3,128,512]{1,2,0:T(8,128)(2,1)S(1)} %copy.101), channel_id=1, source_target_pairs={{0,1},{1,2},{2,3},{3,0},{4,5},{5,6},{6,7},{7,4},{8,9},{9,10},{10,1... | collective-permute-start | bytes 1179656 | tf_op jit(solution)/shard_map/while/body/eval_jaxpr/ppermute | solution.py:12
  78.9 6.3 %collective-permute-start.1 = (f32[128,512]{0,1:T(8,128)S(1)}, f32[128,512]{0,1:T(8,128)S(1)}, u32[]{:S(2)}, u32[]{:S(2)}) collective-permute-start(f32[128,512]{0,1:T(8,128)S(1)} %get-tuple-element.1444), channel_id=1, source_target_pairs={{0,1},{1,2},{2,3},{3,0},{4,5},{5,6},{6,7},{7,4},{8,9},{9,10},{10,1... | collective-permute-start | bytes 786440 | tf_op jit(solution)/shard_map/while/body/eval_jaxpr/ppermute | solution.py:12
  79.9 5.4 %collective-permute-start.2 = (f32[1,4,128]{2,1,0:T(4,128)S(1)}, f32[1,4,128]{2,1,0:T(4,128)S(1)}, u32[]{:S(2)}, u32[]{:S(2)}) collective-permute-start(f32[1,4,128]{2,1,0:T(4,128)S(1)} %get-tuple-element.1678), channel_id=1, source_target_pairs={{0,1},{1,2},{2,3},{3,0},{4,5},{5,6},{6,7},{7,4},{8,9},{9,10},{10,1... | collective-permute-start | bytes 6152 | tf_op jit(solution)/shard_map/while/body/eval_jaxpr/ppermute | solution.py:12
  85.4 15.2 %collective-permute-start = (bf16[3,128,512]{1,2,0:T(8,128)(2,1)S(1)}, bf16[3,128,512]{1,2,0:T(8,128)(2,1)S(1)}, u32[]{:S(2)}, u32[]{:S(2)}) collective-permute-start(bf16[3,128,512]{1,2,0:T(8,128)(2,1)S(1)} %copy.101), channel_id=1, source_target_pairs={{0,1},{1,2},{2,3},{3,0},{4,5},{5,6},{6,7},{7,4},{8,9},{9,10},{10,1... | collective-permute-start | bytes 1179656 | tf_op jit(solution)/shard_map/while/body/eval_jaxpr/ppermute | solution.py:12
  94.7 5.8 %collective-permute-start.1 = (f32[128,512]{0,1:T(8,128)S(1)}, f32[128,512]{0,1:T(8,128)S(1)}, u32[]{:S(2)}, u32[]{:S(2)}) collective-permute-start(f32[128,512]{0,1:T(8,128)S(1)} %get-tuple-element.1444), channel_id=1, source_target_pairs={{0,1},{1,2},{2,3},{3,0},{4,5},{5,6},{6,7},{7,4},{8,9},{9,10},{10,1... | collective-permute-start | bytes 786440 | tf_op jit(solution)/shard_map/while/body/eval_jaxpr/ppermute | solution.py:12
  95.6 4.9 %collective-permute-start.2 = (f32[1,4,128]{2,1,0:T(4,128)S(1)}, f32[1,4,128]{2,1,0:T(4,128)S(1)}, u32[]{:S(2)}, u32[]{:S(2)}) collective-permute-start(f32[1,4,128]{2,1,0:T(4,128)S(1)} %get-tuple-element.1678), channel_id=1, source_target_pairs={{0,1},{1,2},{2,3},{3,0},{4,5},{5,6},{6,7},{7,4},{8,9},{9,10},{10,1... | collective-permute-start | bytes 6152 | tf_op jit(solution)/shard_map/while/body/eval_jaxpr/ppermute | solution.py:12
  108.9 5.8 %collective-permute-start.3 = (f32[128,512]{1,0:T(8,128)S(1)}, f32[128,512]{1,0:T(8,128)S(1)}, u32[]{:S(2)}, u32[]{:S(2)}) collective-permute-start(f32[128,512]{1,0:T(8,128)S(1)} %copy.66), channel_id=1, source_target_pairs={{0,1},{1,2},{2,3},{3,0},{4,5},{5,6},{6,7},{7,4},{8,9},{9,10},{10,1... | collective-permute-start | bytes 786440 | tf_op jit(solution)/shard_map/ppermute | solution.py:12
Sparse Core Ops, SparseCore 0:
  108.9 65.3 reduce-scatter.1
where the time goes:
time: 184 us; the launch traced here: 183 us
  waiting for transfers between devices  80.3 us (44%)
  blocking collectives  43.3 us (24%)
  between operations  14.8 us (8%)
  loops' own time  14.6 us (8%)
  local copies, waits for them, and re-layouts  14.4 us (8%)
  other arithmetic  9.58 us (5%)
  starting transfers between devices  3.4 us (2%)
  matrix products  2.9 us (2%)
    reduce_scatter x1, waiting for transfers between devices, shards(): lax.psum_scatter(key_grads, 'pb', scatter_dimension=0, tiled=True)  59.6 us
    all_gather x1, blocking collectives, shards(): column_keys = lax.all_gather(key_pairs, 'pb', axis=0, tiled=True)  31.9 us
    ppermute x10, waiting for transfers between devices, passed_along(): return lax.ppermute(value, axis, pairs)  20.7 us
    another operation x4, loops' own time, visit_block(): return lax.fori_loop(0, live_tiles, one_tile, (query_grad, key_grads))  14.3 us
    unnamed x21, local copies, waits for them, and re-layouts  6.74 us
    unnamed x1, blocking collectives  6.38 us
    reduce_sum x4, other arithmetic, visit_block(): live_tiles = jnp.sum(wanted.astype(jnp.int32))  5.18 us
    all_gather x1, blocking collectives, shards(): lax.all_gather(selected, 'ka', axis=0, tiled=True)  5.05 us
  transfers between devices with their start and end apart: 11, of which 5 were waited for; matrix products, arithmetic and copies ran while one was open for 7% of the time, Pallas kernels for 0%

commit v1 on v0

--- a/solution.py
+++ b/solution.py
@@ -4,6 +4,24 @@
 from jax.sharding import PartitionSpec as P
 
 VERY_LOW = -1e30
+
+
+def in_order(blocks, dim):
+    blocks = jnp.moveaxis(blocks, 0, dim)
+    shape = blocks.shape
+    return blocks.reshape(*shape[:dim], shape[dim] * shape[dim + 1], *shape[dim + 2 :])
+
+
+def grow_blocks(shard, axis):
+    devices = lax.axis_size(axis)
+    pieces = shard[None]
+    for level in range(devices.bit_length() - 1):
+        distance = 1 << level
+        partner_block = lax.ppermute(pieces, axis, [(i, i ^ distance) for i in range(devices)])
+        both = jnp.stack([pieces, partner_block])
+        upper = lax.axis_index(axis) >> level & 1
+        pieces = jnp.where(upper == 0, both, both[::-1]).reshape(-1, *shard.shape)
+    return pieces
 
 
 def passed_along(value, axis, steps):
@@ -29,7 +47,7 @@
     block_rows = query_rows.shape[0] // block_count
     score_scale = head_width ** (-0.5)
     key_pairs = jnp.concatenate([key_rows, value_rows], 1)
-    column_keys = lax.all_gather(key_pairs, "pb", axis=0, tiled=True)
+    column_keys = in_order(grow_blocks(key_pairs, "pb"), 0)
     peer_slots, peer_counts = (
         lax.all_gather(selected, "ka", axis=0, tiled=True),
         lax.all_gather(counts, "ka", axis=0, tiled=True),

time: 184 us -> 169 us (0.918)
  blocking collectives: 43.3 us -> 9.95 us
  waiting for transfers between devices: 80.3 us -> 91.3 us
  starting transfers between devices: 3.4 us -> 10.8 us
    all_gather x1 -> x0, blocking collectives: 31.9 us -> none  [shards(): column_keys = lax.all_gather(key_pairs, 'pb', axis=0, tiled=True)]
    ppermute x0 -> x3, waiting for transfers between devices: none -> 12.3 us  [grow_blocks(): lax.ppermute(pieces, axis, [(i, i ^ distance) for i in range(devices)])]
    ppermute x0 -> x3, starting transfers between devices: none -> 7.36 us  [grow_blocks(): lax.ppermute(pieces, axis, [(i, i ^ distance) for i in range(devices)])]
    unnamed x21 -> x22, local copies, waits for them, and re-layouts: 6.74 us -> 6.6 us
  transfers between devices with their start and end apart: 11 -> 14, of which waited for: 5 -> 7; matrix products, arithmetic and copies ran while one was open for 7% -> 10% of each run, Pallas kernels for 0% -> 0%
where the time goes in v1:
time: 169 us; the launch traced here: 168 us
  waiting for transfers between devices  91.3 us (54%)
  between operations  14.9 us (9%)
  local copies, waits for them, and re-layouts  14.1 us (8%)
  loops' own time  14 us (8%)
  starting transfers between devices  10.8 us (6%)
  other arithmetic  9.98 us (6%)
  blocking collectives  9.95 us (6%)
  matrix products  2.91 us (2%)
    reduce_scatter x1, waiting for transfers between devices, shards(): lax.psum_scatter(key_grads, 'pb', scatter_dimension=0, tiled=True)  58.2 us
    ppermute x10, waiting for transfers between devices, passed_along(): return lax.ppermute(value, axis, pairs)  20.7 us
    another operation x4, loops' own time, visit_block(): return lax.fori_loop(0, live_tiles, one_tile, (query_grad, key_grads))  13.7 us
    ppermute x3, waiting for transfers between devices, grow_blocks(): lax.ppermute(pieces, axis, [(i, i ^ distance) for i in range(devices)])  12.3 us
    ppermute x3, starting transfers between devices, grow_blocks(): lax.ppermute(pieces, axis, [(i, i ^ distance) for i in range(devices)])  7.36 us
    unnamed x22, local copies, waits for them, and re-layouts  6.6 us
    reduce_sum x4, other arithmetic, visit_block(): live_tiles = jnp.sum(wanted.astype(jnp.int32))  5.3 us
    all_gather x1, blocking collectives, shards(): lax.all_gather(selected, 'ka', axis=0, tiled=True)  5.05 us
  transfers between devices with their start and end apart: 14, of which 7 were waited for; matrix products, arithmetic and copies ran while one was open for 10% of the time, Pallas kernels for 0%

profile of v1, /device:TPU:0, one launch (start us, length us, event | category | flops | bytes accessed | tf_op | source)
XLA Modules:
  0.0 167.9 jit_solution(4759237441835660506)
XLA Ops:
  7.2 0.8 constant_dynamic-update-slice_fusion.1
  8.0 3.1 %collective-permute-start.3 = (bf16[1,128,256]{2,1,0:T(8,128)(2,1)S(1)}, bf16[1,128,256]{2,1,0:T(8,128)(2,1)S(1)}, u32[]{:S(2)}, u32[]{:S(2)}) collective-permute-start(bf16[1,128,256]{2,1,0:T(8,128)(2,1)S(1)} %bitcast.236), channel_id=1, source_target_pairs={{0,4},{4,0},{8,12},{12,8},{16,20},{20,16},{24,28},{28,24},{1,5},{5... | collective-permute-start | bytes 196616 | tf_op jit(solution)/shard_map/ppermute | solution.py:20
  13.0 0.8 dynamic-update-slice
  13.7 4.9 %all-reduce = s32[4]{0:T(128)S(1)} all-reduce(s32[4]{0:T(128)S(1)} %dynamic-update-slice), channel_id=1, replica_groups=mesh['pb'=8,'ka'=4] {'ka'}, use_global_device_ids=true, to_apply=%add | all-reduce | flops 4 | bytes 32
  18.6 0.7 copy-done.5
  19.3 5.0 %all-gather = s32[4,1,2]{2,1,0:T(1,128)S(1)} all-gather(s32[1,1,2]{2,1,0:T(1,128)S(1)} %bitcast.242), channel_id=1, replica_groups=mesh['pb'=8,'ka'=4] {'ka'}, dimensions={0}, use_global_device_ids=true | all-gather | bytes 40 | tf_op jit(solution)/shard_map/all_gather | solution.py:52
  24.9 0.7 and_convert_fusion
  25.8 1.6 collective-permute-start.4
  27.5 4.2 %collective-permute-done.4 = bf16[2,128,256]{2,1,0:T(8,128)(2,1)S(1)} collective-permute-done((bf16[2,128,256]{2,1,0:T(8,128)(2,1)S(1)}, bf16[2,128,256]{2,1,0:T(8,128)(2,1)S(1)}, u32[]{:S(2)}, u32[]{:S(2)}) %collective-permute-start.4) | collective-permute-done | bytes 131104 | tf_op jit(solution)/shard_map/ppermute | solution.py:20
  31.7 2.7 %collective-permute-start.5 = (bf16[4,128,256]{2,1,0:T(8,128)(2,1)S(1)}, bf16[4,128,256]{2,1,0:T(8,128)(2,1)S(1)}, u32[]{:S(2)}, u32[]{:S(2)}) collective-permute-start(bf16[4,128,256]{2,1,0:T(8,128)(2,1)S(1)} %bitcast.228), channel_id=1, source_target_pairs={{0,16},{4,20},{8,24},{12,28},{16,0},{20,4},{24,8},{28,12},{1,17},{... | collective-permute-start | bytes 786440 | tf_op jit(solution)/shard_map/ppermute | solution.py:20
  34.4 1.4 convert_reduce_fusion.1
  35.9 0.8 copy-done.2
  36.8 0.8 copy-done.3
  37.8 8.2 %collective-permute-done.5 = bf16[4,128,256]{2,1,0:T(8,128)(2,1)S(1)} collective-permute-done((bf16[4,128,256]{2,1,0:T(8,128)(2,1)S(1)}, bf16[4,128,256]{2,1,0:T(8,128)(2,1)S(1)}, u32[]{:S(2)}, u32[]{:S(2)}) %collective-permute-start.5) | collective-permute-done | bytes 262176 | tf_op jit(solution)/shard_map/ppermute | solution.py:20
  46.9 39.9 %while.86 = (s32[]{:T(128)}, bf16[3,128,512]{1,2,0:T(8,128)(2,1)S(1)}, f32[128,512]{0,1:T(8,128)S(1)}, f32[1,4,128]{2,1,0:T(4,128)S(1)}, f32[1024,256]{0,1:T(8,1...) while((s32[]{:T(128)}, ...), condition=%wide.region_7.8_spmd.clone.clone, body=%wide.region_0.7_spmd.clone.clone.sunk | while | flops 84836216 | bytes 8673559 | solution.py:148
  47.6 1.3 convert_reduce_fusion.3
  49.9 5.9 %while.88 = (s32[]{:T(128)}, f32[128,512]{0,1:T(8,128)S(1)}, f32[1024,256]{0,1:T(8,128)S(1)}, s32[]{:T(128)}, s32[2]{0:T(128)S(1)}, /*index=5*/bf16[1024,256]{1,...) while((s32[]{:T(128)}, f32[128,512]{0,1:T(8,128)S(1)}, ...), condition=%wide.region_6.6_spmd.clone, body=%wide.region_5.5_spmd.clone.sunk | while | flops 84574488 | bytes 3415011 | solution.py:132
  55.8 1.0 collective-permute-start.1
  56.9 4.8 %collective-permute-done.1 = f32[128,512]{0,1:T(8,128)S(1)} collective-permute-done((f32[128,512]{0,1:T(8,128)S(1)}, f32[128,512]{0,1:T(8,128)S(1)}, u32[]{:S(2)}, u32[]{:S(2)}) %collective-permute-start.1) | collective-permute-done | bytes 262176 | tf_op jit(solution)/shard_map/while/body/eval_jaxpr/ppermute | solution.py:30
  62.5 1.3 convert_reduce_fusion.3
  65.4 1.0 collective-permute-start.1
  66.5 5.3 %collective-permute-done.1 = f32[128,512]{0,1:T(8,128)S(1)} collective-permute-done((f32[128,512]{0,1:T(8,128)S(1)}, f32[128,512]{0,1:T(8,128)S(1)}, u32[]{:S(2)}, u32[]{:S(2)}) %collective-permute-start.1) | collective-permute-done | bytes 262176 | tf_op jit(solution)/shard_map/while/body/eval_jaxpr/ppermute | solution.py:30
  72.6 1.3 convert_reduce_fusion.3
  75.0 5.9 %while.88 = (s32[]{:T(128)}, f32[128,512]{0,1:T(8,128)S(1)}, f32[1024,256]{0,1:T(8,128)S(1)}, s32[]{:T(128)}, s32[2]{0:T(128)S(1)}, /*index=5*/bf16[1024,256]{1,...) while((s32[]{:T(128)}, f32[128,512]{0,1:T(8,128)S(1)}, ...), condition=%wide.region_6.6_spmd.clone, body=%wide.region_5.5_spmd.clone.sunk | while | flops 84574488 | bytes 3415011 | solution.py:132
  80.9 1.0 collective-permute-start.1
  81.9 4.8 %collective-permute-done.1 = f32[128,512]{0,1:T(8,128)S(1)} collective-permute-done((f32[128,512]{0,1:T(8,128)S(1)}, f32[128,512]{0,1:T(8,128)S(1)}, u32[]{:S(2)}, u32[]{:S(2)}) %collective-permute-start.1) | collective-permute-done | bytes 262176 | tf_op jit(solution)/shard_map/while/body/eval_jaxpr/ppermute | solution.py:30
  86.9 6.5 %while.87 = (s32[]{:T(128)}, f32[128,512]{0,1:T(8,128)S(1)}, f32[1024,256]{0,1:T(8,128)S(1)}, s32[]{:T(128)}, s32[2]{0:T(128)S(1)}, /*index=5*/bf16[1024,256]{1,...) while((s32[]{:T(128)}, f32[128,512]{0,1:T(8,128)S(1)}, ...), condition=%wide.region_13.14_spmd.clone.clone, body=%wide.region_12.13_spmd.clone.clone.sunk | while | flops 84574488 | bytes 3414491 | solution.py:132
  93.3 1.3 copy.67
  94.9 5.8 %collective-permute-done.6 = f32[128,512]{1,0:T(8,128)S(1)} collective-permute-done((f32[128,512]{1,0:T(8,128)S(1)}, f32[128,512]{1,0:T(8,128)S(1)}, u32[]{:S(2)}, u32[]{:S(2)}) %collective-permute-start.6) | collective-permute-done | bytes 262176 | tf_op jit(solution)/shard_map/ppermute | solution.py:30
  100.7 58.2 %reduce-scatter.2.cloned.1.call-done = f32[128,256]{1,0:T(8,128)} async-done(((f32[1024,256]{1,0:T(8,128)}), f32[128,256]{1,0:T(8,128)}) %reduce-scatter.2.cloned.1.call-update) | async-done | bytes 131088 | tf_op jit(solution)/shard_map/reduce_scatter | solution.py:155
  158.8 1.5 fusion.45
  160.4 0.7 copy.126
  (117 shorter events, 14.9 us)
Async XLA Ops:
  7.2 151.7 %reduce-scatter.2.cloned.1.call-start = ((), (), s32[]{:S(2)}) async-start(), calls=%async_computation.1 | async-start | bytes 1179648 | tf_op jit(solution)/shard_map/reduce_scatter | solution.py:155
  7.2 0.8 copy-start.4
  8.0 17.8 %collective-permute-start.3 = (bf16[1,128,256]{2,1,0:T(8,128)(2,1)S(1)}, bf16[1,128,256]{2,1,0:T(8,128)(2,1)S(1)}, u32[]{:S(2)}, u32[]{:S(2)}) collective-permute-start(bf16[1,128,256]{2,1,0:T(8,128)(2,1)S(1)} %bitcast.236), channel_id=1, source_target_pairs={{0,4},{4,0},{8,12},{12,8},{16,20},{20,16},{24,28},{28,24},{1,5},{5... | collective-permute-start | bytes 196616 | tf_op jit(solution)/shard_map/ppermute | solution.py:20
  11.7 0.7 copy-start.6
  18.6 0.7 copy-start.5
  25.8 5.8 %collective-permute-start.4 = (bf16[2,128,256]{2,1,0:T(8,128)(2,1)S(1)}, bf16[2,128,256]{2,1,0:T(8,128)(2,1)S(1)}, u32[]{:S(2)}, u32[]{:S(2)}) collective-permute-start(bf16[2,128,256]{2,1,0:T(8,128)(2,1)S(1)} %get-tuple-element.1225), channel_id=1, source_target_pairs={{0,8},{4,12},{8,0},{12,4},{16,24},{20,28},{24,16},{28,20},{1,9},{5... | collective-permute-start | bytes 393224 | tf_op jit(solution)/shard_map/ppermute | solution.py:20
  31.7 4.1 %copy-start.1 = (bf16[128,512]{1,0:T(8,128)(2,1)S(1)}, bf16[128,512]{1,0:T(8,128)(2,1)}, u32[]{:S(2)}) copy-start(bf16[128,512]{1,0:T(8,128)(2,1)} %param.17) | copy-start | bytes 393220
  31.7 14.3 %collective-permute-start.5 = (bf16[4,128,256]{2,1,0:T(8,128)(2,1)S(1)}, bf16[4,128,256]{2,1,0:T(8,128)(2,1)S(1)}, u32[]{:S(2)}, u32[]{:S(2)}) collective-permute-start(bf16[4,128,256]{2,1,0:T(8,128)(2,1)S(1)} %bitcast.228), channel_id=1, source_target_pairs={{0,16},{4,20},{8,24},{12,28},{16,0},{20,4},{24,8},{28,12},{1,17},{... | collective-permute-start | bytes 786440 | tf_op jit(solution)/shard_map/ppermute | solution.py:20
  35.8 0.9 copy-start.2
  36.7 0.9 copy-start.3
  46.2 0.7 copy-start
  46.9 14.8 %collective-permute-start = (bf16[3,128,512]{1,2,0:T(8,128)(2,1)S(1)}, bf16[3,128,512]{1,2,0:T(8,128)(2,1)S(1)}, u32[]{:S(2)}, u32[]{:S(2)}) collective-permute-start(bf16[3,128,512]{1,2,0:T(8,128)(2,1)S(1)} %copy.102), channel_id=1, source_target_pairs={{0,1},{1,2},{2,3},{3,0},{4,5},{5,6},{6,7},{7,4},{8,9},{9,10},{10,1... | collective-permute-start | bytes 1179656 | tf_op jit(solution)/shard_map/while/body/eval_jaxpr/ppermute | solution.py:30
  55.8 5.8 %collective-permute-start.1 = (f32[128,512]{0,1:T(8,128)S(1)}, f32[128,512]{0,1:T(8,128)S(1)}, u32[]{:S(2)}, u32[]{:S(2)}) collective-permute-start(f32[128,512]{0,1:T(8,128)S(1)} %get-tuple-element.1446), channel_id=1, source_target_pairs={{0,1},{1,2},{2,3},{3,0},{4,5},{5,6},{6,7},{7,4},{8,9},{9,10},{10,1... | collective-permute-start | bytes 786440 | tf_op jit(solution)/shard_map/while/body/eval_jaxpr/ppermute | solution.py:30
  56.8 4.9 %collective-permute-start.2 = (f32[1,4,128]{2,1,0:T(4,128)S(1)}, f32[1,4,128]{2,1,0:T(4,128)S(1)}, u32[]{:S(2)}, u32[]{:S(2)}) collective-permute-start(f32[1,4,128]{2,1,0:T(4,128)S(1)} %get-tuple-element.1680), channel_id=1, source_target_pairs={{0,1},{1,2},{2,3},{3,0},{4,5},{5,6},{6,7},{7,4},{8,9},{9,10},{10,1... | collective-permute-start | bytes 6152 | tf_op jit(solution)/shard_map/while/body/eval_jaxpr/ppermute | solution.py:30
  61.8 10.1 %collective-permute-start = (bf16[3,128,512]{1,2,0:T(8,128)(2,1)S(1)}, bf16[3,128,512]{1,2,0:T(8,128)(2,1)S(1)}, u32[]{:S(2)}, u32[]{:S(2)}) collective-permute-start(bf16[3,128,512]{1,2,0:T(8,128)(2,1)S(1)} %copy.102), channel_id=1, source_target_pairs={{0,1},{1,2},{2,3},{3,0},{4,5},{5,6},{6,7},{7,4},{8,9},{9,10},{10,1... | collective-permute-start | bytes 1179656 | tf_op jit(solution)/shard_map/while/body/eval_jaxpr/ppermute | solution.py:30
  65.4 6.4 %collective-permute-start.1 = (f32[128,512]{0,1:T(8,128)S(1)}, f32[128,512]{0,1:T(8,128)S(1)}, u32[]{:S(2)}, u32[]{:S(2)}) collective-permute-start(f32[128,512]{0,1:T(8,128)S(1)} %get-tuple-element.1446), channel_id=1, source_target_pairs={{0,1},{1,2},{2,3},{3,0},{4,5},{5,6},{6,7},{7,4},{8,9},{9,10},{10,1... | collective-permute-start | bytes 786440 | tf_op jit(solution)/shard_map/while/body/eval_jaxpr/ppermute | solution.py:30
  66.4 5.4 %collective-permute-start.2 = (f32[1,4,128]{2,1,0:T(4,128)S(1)}, f32[1,4,128]{2,1,0:T(4,128)S(1)}, u32[]{:S(2)}, u32[]{:S(2)}) collective-permute-start(f32[1,4,128]{2,1,0:T(4,128)S(1)} %get-tuple-element.1680), channel_id=1, source_target_pairs={{0,1},{1,2},{2,3},{3,0},{4,5},{5,6},{6,7},{7,4},{8,9},{9,10},{10,1... | collective-permute-start | bytes 6152 | tf_op jit(solution)/shard_map/while/body/eval_jaxpr/ppermute | solution.py:30
  71.9 14.8 %collective-permute-start = (bf16[3,128,512]{1,2,0:T(8,128)(2,1)S(1)}, bf16[3,128,512]{1,2,0:T(8,128)(2,1)S(1)}, u32[]{:S(2)}, u32[]{:S(2)}) collective-permute-start(bf16[3,128,512]{1,2,0:T(8,128)(2,1)S(1)} %copy.102), channel_id=1, source_target_pairs={{0,1},{1,2},{2,3},{3,0},{4,5},{5,6},{6,7},{7,4},{8,9},{9,10},{10,1... | collective-permute-start | bytes 1179656 | tf_op jit(solution)/shard_map/while/body/eval_jaxpr/ppermute | solution.py:30
  80.9 5.8 %collective-permute-start.1 = (f32[128,512]{0,1:T(8,128)S(1)}, f32[128,512]{0,1:T(8,128)S(1)}, u32[]{:S(2)}, u32[]{:S(2)}) collective-permute-start(f32[128,512]{0,1:T(8,128)S(1)} %get-tuple-element.1446), channel_id=1, source_target_pairs={{0,1},{1,2},{2,3},{3,0},{4,5},{5,6},{6,7},{7,4},{8,9},{9,10},{10,1... | collective-permute-start | bytes 786440 | tf_op jit(solution)/shard_map/while/body/eval_jaxpr/ppermute | solution.py:30
  81.8 4.9 %collective-permute-start.2 = (f32[1,4,128]{2,1,0:T(4,128)S(1)}, f32[1,4,128]{2,1,0:T(4,128)S(1)}, u32[]{:S(2)}, u32[]{:S(2)}) collective-permute-start(f32[1,4,128]{2,1,0:T(4,128)S(1)} %get-tuple-element.1680), channel_id=1, source_target_pairs={{0,1},{1,2},{2,3},{3,0},{4,5},{5,6},{6,7},{7,4},{8,9},{9,10},{10,1... | collective-permute-start | bytes 6152 | tf_op jit(solution)/shard_map/while/body/eval_jaxpr/ppermute | solution.py:30
  94.8 5.8 %collective-permute-start.6 = (f32[128,512]{1,0:T(8,128)S(1)}, f32[128,512]{1,0:T(8,128)S(1)}, u32[]{:S(2)}, u32[]{:S(2)}) collective-permute-start(f32[128,512]{1,0:T(8,128)S(1)} %copy.66), channel_id=1, source_target_pairs={{0,1},{1,2},{2,3},{3,0},{4,5},{5,6},{6,7},{7,4},{8,9},{9,10},{10,1... | collective-permute-start | bytes 786440 | tf_op jit(solution)/shard_map/ppermute | solution.py:30
Sparse Core Ops, SparseCore 0:
  94.8 64.0 reduce-scatter.1
